TPU v7x, 32 devices: a whole 2x2x4 slice. The times are simulated.
32 devices in a mesh: row: 8 (over z, y), col: 4 (over x, core).
Axes of the slice: x: 2, y: 2, z: 4, core: 2. Of those that a mesh axis runs over, the one named last changes fastest.
Arguments:
- tokens: bfloat16 [1600, 8192], P('row', 'col')
- ln1_gain: float32 [1600], P('row'), may hold values from 0.25 to 1.75
- ln1_shift: float32 [1600], P('row'), may hold values from -4 to 4
- weight_qkv: bfloat16 [1600, 4800], P('row', 'col'), may hold values from -0.21875 to 0.21875
- bias_qkv: float32 [4800], P('col'), may hold values from -4 to 4
- weight_out: bfloat16 [1600, 1600], P('row', 'col'), may hold values from -0.625 to 0.625
- bias_out: float32 [1600], P('row'), may hold values from -6 to 6
- ln2_gain: float32 [1600], P('row'), may hold values from 0.25 to 1.75
- ln2_shift: float32 [1600], P('row'), may hold values from -4 to 4
- weight_up: bfloat16 [1600, 6400], P('row', 'col'), may hold values from -0.15625 to 0.15625
- bias_up: float32 [6400], P('col'), may hold values from -6 to 6
- weight_down: bfloat16 [1600, 6400], P('row', 'col'), may hold values from -0.109375 to 0.109375
- bias_down: float32 [1600], P('row'), may hold values from -6 to 6
- cotangent: bfloat16 [1600, 8192], P('row', 'col')
Outputs:
- block_output: bfloat16 [1600, 8192], P('row', 'col')
- grad_tokens: float32 [1600, 8192], P('row', 'col')
- grad_ln1_gain: float32 [1600], P('row')
- grad_ln1_shift: float32 [1600], P('row')
- grad_weight_qkv: float32 [1600, 4800], P('row', 'col')
- grad_bias_qkv: float32 [4800], P('col')
- grad_weight_out: float32 [1600, 1600], P('row', 'col')
- grad_bias_out: float32 [1600], P('row')
- grad_ln2_gain: float32 [1600], P('row')
- grad_ln2_shift: float32 [1600], P('row')
- grad_weight_up: float32 [1600, 6400], P('row', 'col')
- grad_bias_up: float32 [6400], P('col')
- grad_weight_down: float32 [1600, 6400], P('row', 'col')
- grad_bias_down: float32 [1600], P('row')
All inputs are finite; a program needn't handle non-finite values.
Results may differ from a plain program's by a relative error of at most 0.012.
The roundings to bfloat16 on the way count: a program that leaves them out, or rounds other values in their place, can miss the bound.
Values may be sent and summed in bfloat16 or wider, within the bound.
A program may use at most 256 MiB of HBM per device.

v0:
```python
import jax
import jax.numpy as jnp
from jax import lax
from jax.sharding import PartitionSpec as P

D = 1600
H = 25
HD = 64
L = 1024
CHANNELS = 3 * HD
epsilon = 1e-05
excluded = -1e30
TN = (((0,), (0,)), ((), ()))
NN = (((1,), (0,)), ((), ()))
NT = (((1,), (1,)), ((), ()))


def product(left, right, dims):
    return lax.dot_general(left, right, dims, preferred_element_type=jnp.float32)


def norm_stats(values):
    mean = jnp.mean(values, axis=0, keepdims=True)
    centred = values - mean
    scale = lax.rsqrt(jnp.mean(centred * centred, axis=0, keepdims=True) + epsilon)
    return (centred * scale, scale)


def norm_backward(gradient, centred, scale, gain):
    scaled = gradient * gain
    adjusted = (
        scaled
        - jnp.mean(scaled, axis=0, keepdims=True)
        - centred * jnp.mean(scaled * centred, axis=0, keepdims=True)
    )
    return (adjusted * scale, jnp.sum(gradient * centred, axis=1), jnp.sum(gradient, axis=1))


def block_order(rows, cols):
    return [(q * cols + c, c * rows + q) for q in range(rows) for c in range(cols)]


def to_blocks(values, rows, cols):
    k, feats, toks = values.shape
    split = values.reshape(k, feats, rows, toks // rows)
    got = lax.all_to_all(split, "row", split_axis=2, concat_axis=1)
    got = got.reshape(k, rows * feats, toks // rows)
    return lax.ppermute(got, ("row", "col"), block_order(rows, cols))


def from_blocks(values, rows, cols):
    back = [(b, a) for a, b in block_order(rows, cols)]
    got = lax.ppermute(values, ("row", "col"), back)
    feats, toks = values.shape
    got = got.reshape(rows, feats // rows, toks)
    got = lax.all_to_all(got, "row", split_axis=0, concat_axis=1)
    return got.reshape(feats // rows, rows * toks)


def regroup_matrix(channels, slots, cols):
    source = jnp.arange(channels * H, dtype=jnp.int32)
    channel, head = (source // H, source % H)
    target = (head % cols * slots + head // cols) * channels + channel
    return (
        target[:, None] == jnp.arange(cols * slots * channels, dtype=jnp.int32)[None, :]
    ).astype(jnp.bfloat16)


def group_heads(weight, matrix, cols):
    moved = product(weight, matrix, NN).astype(jnp.bfloat16)
    moved = moved.reshape(moved.shape[0], cols, -1)
    got = lax.all_to_all(moved, "col", split_axis=1, concat_axis=1, tiled=True)
    return got.reshape(got.shape[0], -1)


def ungroup_heads(gradient, matrix, cols):
    moved = gradient.reshape(gradient.shape[0], cols, -1)
    got = lax.all_to_all(moved, "col", split_axis=1, concat_axis=1, tiled=True)
    return product(got.reshape(got.shape[0], -1), matrix, NT)


def head_rows(values, cols, slots):
    rest = values.shape[1:]
    split = values.reshape(cols, slots, -1, *rest)
    return jnp.moveaxis(split, 0, 1).reshape(slots, -1, *rest)


def flat_rows(values, cols, slots):
    rest = values.shape[2:]
    split = values.reshape(slots, cols, -1, *rest)
    return jnp.moveaxis(split, 0, 1).reshape(-1, *rest)


def attend_forward(heads):
    allowed = jnp.arange(L)[:, None] <= jnp.arange(L)[None, :]
    outs, logs = ([], [])
    for s in range(heads.shape[0]):
        query, key, value = (heads[s, :HD], heads[s, HD : 2 * HD], heads[s, 2 * HD :])
        scores = product(key, query, TN) * HD ** (-0.5)
        scores = jnp.where(allowed, scores, excluded)
        peak = jnp.max(scores, axis=0, keepdims=True)
        weights = jnp.exp(scores - peak)
        total = jnp.sum(weights, axis=0, keepdims=True)
        low = (weights / total).astype(jnp.bfloat16)
        outs.append(product(value, low, NN).astype(jnp.bfloat16))
        logs.append(peak + jnp.log(total))
    return (jnp.stack(outs), jnp.stack(logs))


def attend_backward(heads, grads, logs):
    allowed = jnp.arange(L)[:, None] <= jnp.arange(L)[None, :]
    outs = []
    for s in range(heads.shape[0]):
        query, key, value = (heads[s, :HD], heads[s, HD : 2 * HD], heads[s, 2 * HD :])
        grad = grads[s]
        scores = product(key, query, TN) * HD ** (-0.5)
        scores = jnp.where(allowed, scores, excluded)
        weights = jnp.exp(scores - logs[s])
        grad_value = product(grad, weights.astype(jnp.bfloat16), NT)
        grad_weights = product(value, grad, TN)
        inner = jnp.sum(weights * grad_weights, axis=0, keepdims=True)
        low = (weights * (grad_weights - inner)).astype(jnp.bfloat16)
        grad_query = product(key, low, NN) * HD ** (-0.5)
        grad_key = product(query, low, NT) * HD ** (-0.5)
        outs.append(
            jnp.concatenate([grad_query, grad_key, grad_value], axis=0).astype(jnp.bfloat16)
        )
    return jnp.stack(outs)


def spread(values):
    return lax.all_gather(values, "col", axis=1, tiled=True)


def share(values):
    return lax.psum_scatter(
        values.astype(jnp.bfloat16), "col", scatter_dimension=1, tiled=True
    ).astype(jnp.float32)


def whole_weight(weight):
    return lax.all_gather(weight, "row", axis=0, tiled=True)


def share_weight(gradient):
    return lax.psum_scatter(gradient.astype(jnp.bfloat16), "row", scatter_dimension=0, tiled=True)


def body(
    tokens,
    ln1_gain,
    ln1_shift,
    weight_qkv,
    bias_qkv,
    weight_out,
    bias_out,
    ln2_gain,
    ln2_shift,
    weight_up,
    bias_up,
    weight_down,
    bias_down,
    cotangent,
):
    rows, cols = (lax.axis_size("row"), lax.axis_size("col"))
    row, col = (lax.axis_index("row"), lax.axis_index("col"))
    slots = (H + cols - 1) // cols
    qkv_channels = CHANNELS // cols
    out_channels = HD // cols
    vectors = lax.all_gather(
        jnp.stack([ln1_gain, ln1_shift, bias_out, ln2_gain, ln2_shift, bias_down]),
        "row",
        axis=1,
        tiled=True,
    )[:, :, None]
    gain_one, shift_one, out_bias, gain_two, shift_two, down_bias = vectors
    biases = lax.all_gather(bias_qkv, "col", axis=0, tiled=True).reshape(CHANNELS, H)
    biases = jnp.pad(biases, ((0, 0), (0, slots * cols - H))).reshape(CHANNELS, slots, cols)
    qkv_bias = lax.dynamic_index_in_dim(biases, col, axis=2, keepdims=False).T[:, :, None]
    qkv_matrix = regroup_matrix(qkv_channels, slots, cols)
    out_matrix = regroup_matrix(out_channels, slots, cols)
    qkv_weight = whole_weight(group_heads(weight_qkv, qkv_matrix, cols))
    out_weight = whole_weight(group_heads(weight_out, out_matrix, cols))
    up_weight = whole_weight(weight_up)
    down_weight = whole_weight(weight_down)
    own = to_blocks(jnp.stack([tokens, cotangent]), rows, cols)
    both = lax.all_gather(own, "col", axis=2, tiled=True)
    residual_own = own[0].astype(jnp.float32)
    cot_own = own[1].astype(jnp.float32)
    cot = both[1]
    normed_in = (norm_stats(both[0].astype(jnp.float32))[0] * gain_one + shift_one).astype(
        jnp.bfloat16
    )
    qkv = product(qkv_weight, normed_in, TN)
    heads = (head_rows(qkv, cols, slots) + qkv_bias).astype(jnp.bfloat16)
    attended, logs = attend_forward(heads)
    attended = flat_rows(attended, cols, slots)
    residual_mid = residual_own + share(product(out_weight, attended, NN)) + out_bias
    centred_mid, scale_mid = norm_stats(residual_mid)
    normed_mid = spread((centred_mid * gain_two + shift_two).astype(jnp.bfloat16))
    hidden_pre = product(up_weight, normed_mid, TN) + bias_up[:, None]
    hidden = jax.nn.gelu(hidden_pre, approximate=True).astype(jnp.bfloat16)
    block_output = (residual_mid + share(product(down_weight, hidden, NN)) + down_bias).astype(
        jnp.bfloat16
    )
    block_output = from_blocks(block_output, rows, cols)
    grad_hidden = product(down_weight, cot, TN)
    gelu_back = jax.vjp(lambda inner: jax.nn.gelu(inner, approximate=True), hidden_pre)[1]
    grad_pre = gelu_back(grad_hidden)[0].astype(jnp.bfloat16)
    grad_weight_down = share_weight(product(cot, hidden, NT)).astype(jnp.float32)
    grad_normed_mid = share(product(up_weight, grad_pre, NN))
    grad_weight_up = share_weight(product(normed_mid, grad_pre, NT)).astype(jnp.float32)
    up_part = jnp.sum(grad_pre, axis=1, dtype=jnp.float32)
    grad_norm_mid, gain_two_part, shift_two_part = norm_backward(
        grad_normed_mid, centred_mid, scale_mid, gain_two
    )
    grad_residual_mid = cot_own + grad_norm_mid
    grad_branch_own = grad_residual_mid.astype(jnp.bfloat16)
    grad_branch = spread(grad_branch_own)
    grad_attended = product(out_weight, grad_branch, TN).astype(jnp.bfloat16)
    grad_weight_out = ungroup_heads(
        share_weight(product(grad_branch, attended, NT)), out_matrix, cols
    )
    grad_qkv = attend_backward(heads, head_rows(grad_attended, cols, slots), logs)
    grad_qkv = flat_rows(grad_qkv, cols, slots)
    grad_weight_qkv = ungroup_heads(
        share_weight(product(normed_in, grad_qkv, NT)), qkv_matrix, cols
    )
    qkv_part = jnp.sum(grad_qkv, axis=1, dtype=jnp.float32)
    grad_normed_in = share(product(qkv_weight, grad_qkv, NN))
    centred_in, scale_in = norm_stats(residual_own)
    grad_norm_in, gain_one_part, shift_one_part = norm_backward(
        grad_normed_in, centred_in, scale_in, gain_one
    )
    grad_tokens = from_blocks(grad_residual_mid + grad_norm_in, rows, cols)
    features = jnp.stack(
        [
            gain_one_part,
            shift_one_part,
            jnp.sum(grad_branch_own, axis=1, dtype=jnp.float32),
            gain_two_part,
            shift_two_part,
            jnp.sum(cot_own, axis=1),
        ]
    )
    features = lax.psum(features, ("row", "col"))
    features = lax.dynamic_slice_in_dim(features, row * (D // rows), D // rows, axis=1)
    units = lax.psum(jnp.concatenate([up_part, qkv_part]), "row")
    grad_bias_up = units[: up_part.shape[0]]
    spread_bias = lax.all_gather(
        units[up_part.shape[0] :].reshape(cols, slots, qkv_channels), "col", axis=0
    )
    mine = lax.dynamic_index_in_dim(spread_bias, col, axis=1, keepdims=False)
    grad_bias_qkv = mine.transpose(2, 1, 0).reshape(qkv_channels, slots * cols)[:, :H].reshape(-1)
    return (
        block_output,
        grad_tokens,
        features[0],
        features[1],
        grad_weight_qkv,
        grad_bias_qkv,
        grad_weight_out,
        features[2],
        features[3],
        features[4],
        grad_weight_up,
        grad_bias_up,
        grad_weight_down,
        features[5],
    )


def solution(mesh):
    both, row, col = (P("row", "col"), P("row"), P("col"))
    in_specs = (both, row, row, both, col, both, row, row, row, both, col, both, row, both)
    out_specs = (both, both, row, row, both, col, both, row, row, row, both, col, both, row)
    return jax.shard_map(body, mesh=mesh, in_specs=in_specs, out_specs=out_specs, check_vma=False)
```

profile of v0, /device:TPU:14, one launch (start us, length us, event | category | flops | bytes accessed | tf_op | source)
XLA Modules:
  0.0 1462.5 jit_solution(7190868534278760962)
XLA Ops:
  10.5 11.2 all_to_all.65
  24.3 61.1 %all_to_all.66 = bf16[2,1,200,8,256]{4,2,0,1,3:T(8,128)(2,1)S(1)} all-to-all(bf16[2,1,200,8,256]{4,2,0,1,3:T(8,128)(2,1)S(1)} %copy.106), channel_id=1, replica_groups=mesh['row'=8,'col'=4] {'row'}, dimensions={3} | all-to-all | bytes 3276800 | tf_op jit(solution)/shard_map/all_to_all | solution.py:46
  87.9 102.6 %collective-permute-done = bf16[2,1600,256]{2,1,0:T(8,128)(2,1)S(1)} collective-permute-done((bf16[2,1600,256]{2,1,0:T(8,128)(2,1)S(1)}, bf16[2,1600,256]{2,1,0:T(8,128)(2,1)S(1)}, u32[]{:S(2)}, u32[]{:S(2)}) %collective-permute-start) | collective-permute-done | bytes 1638432 | tf_op jit(solution)/shard_map/ppermute | solution.py:48
  193.0 6.0 all-to-all-start.1
  200.6 11.4 all-reduce.1
  212.4 26.7 %all-gather = f32[8,200,6]{1,2,0:T(8,128)S(1)} all-gather(f32[1,200,6]{1,2,0:T(8,128)S(1)} %bitcast.520), channel_id=1, replica_groups=mesh['row'=8,'col'=4] {'row'}, dimensions={0}, use_global_device_ids=true | all-gather | bytes 43200 | tf_op jit(solution)/shard_map/all_gather | solution.py:170
  240.9 7.5 copy.112
  254.4 7.7 fusion.43
  280.9 7.9 all-gather.9.cloned.1.call-done
  294.5 36.7 %reduce-scatter.15.cloned.1.call-done = bf16[1600,256]{1,0:T(8,128)(2,1)} async-done(((bf16[1600,1024]{1,0:T(8,128)(2,1)}), bf16[1600,256]{1,0:T(8,128)(2,1)}) %reduce-scatter.15.cloned.1.call-update) | async-done | bytes 819216 | tf_op jit(solution)/shard_map/reduce_scatter | solution.py:136
  338.4 81.3 %all-gather.17.cloned.1.call-done = bf16[1600,1600]{1,0:T(8,128)(2,1)} async-done(((bf16[200,1600]{1,0:T(8,128)(2,1)}), bf16[1600,1600]{1,0:T(8,128)(2,1)}) %all-gather.17.cloned.1.call-update) | async-done | bytes 5120016 | tf_op jit(solution)/shard_map/all_gather | solution.py:142
  419.7 31.1 %all-gather.15.cloned.1.call-done = bf16[1600,1024]{1,0:T(8,128)(2,1)} async-done(((bf16[1600,256]{1,0:T(8,128)(2,1)}), bf16[1600,1024]{1,0:T(8,128)(2,1)}) %all-gather.15.cloned.1.call-update) | async-done | bytes 3276816 | tf_op jit(solution)/shard_map/all_gather | solution.py:132
  450.8 11.1 fusion.233
  461.9 77.5 %all-gather.19.cloned.1.call-done = bf16[1600,1600]{1,0:T(8,128)(2,1)} async-done(((bf16[200,1600]{1,0:T(8,128)(2,1)}), bf16[1600,1600]{1,0:T(8,128)(2,1)}) %all-gather.19.cloned.1.call-update) | async-done | bytes 5120016 | tf_op jit(solution)/shard_map/all_gather | solution.py:142
  539.4 15.8 %convert_reduce_fusion.1 = (f32[1600]{0:T(1024)}, bf16[1600,1024]{1,0:T(8,128)(2,1)S(1)}) fusion(f32[1024,1600]{0,1:T(8,128)} %fusion.233, f32[1600]{0:T(1024)S(1)} %copy-done.50, bf16[1600,1600]{1,0:T(8,128)(2,1)} %all-gather.19.cloned.1.call-done, bf16[2,1600,1024]{2,1,0:T(8,128)(2,1)} %all-gather.13.cloned.1.call-done), kind=kOutput, calls=%fused_computation.32 | convolution fusion | flops 5280561664 | bytes 18444800 | tf_op jit(solution)/shard_map/dot_general | solution.py:19
  557.0 7.4 fusion.34
  564.9 37.8 %reduce-scatter.19.cloned.1.call-done = bf16[1600,256]{1,0:T(8,128)(2,1)} async-done(((bf16[1600,1024]{1,0:T(8,128)(2,1)}), bf16[1600,256]{1,0:T(8,128)(2,1)}) %reduce-scatter.19.cloned.1.call-update) | async-done | bytes 819216 | tf_op jit(solution)/shard_map/reduce_scatter | solution.py:136
  608.5 29.5 %all-gather.21.cloned.1.call-done = bf16[1600,1024]{1,0:T(8,128)(2,1)} async-done(((bf16[1600,256]{1,0:T(8,128)(2,1)}), bf16[1600,1024]{1,0:T(8,128)(2,1)}) %all-gather.21.cloned.1.call-update) | async-done | bytes 3276816 | tf_op jit(solution)/shard_map/all_gather | solution.py:132
  680.2 6.7 convolution_convert_fusion.5
  687.0 11.5 fusion.33
  704.0 9.7 convolution_convert_fusion.2
  713.9 12.9 convolution_convert_fusion
  726.9 10.3 convolution_convert_fusion.1
  739.6 27.7 %reduce-scatter.17.cloned.1.call-done = bf16[1600,256]{1,0:T(8,128)(2,1)} async-done(((bf16[1600,1024]{1,0:T(8,128)(2,1)}), bf16[1600,256]{1,0:T(8,128)(2,1)}) %reduce-scatter.17.cloned.1.call-update) | async-done | bytes 819216 | tf_op jit(solution)/shard_map/reduce_scatter | solution.py:136
  776.6 95.2 %reduce-scatter.23.cloned.1.call-done = bf16[200,448]{1,0:T(8,128)(2,1)} async-done(((bf16[1600,448]{1,0:T(8,128)(2,1)}), bf16[200,448]{1,0:T(8,128)(2,1)}) %reduce-scatter.23.cloned.1.call-update) | async-done | bytes 179216 | tf_op jit(solution)/shard_map/reduce_scatter | solution.py:146
  873.0 6.9 all_to_all.67
  888.8 192.3 %reduce-scatter.25.cloned.1.call-done = bf16[200,1344]{1,0:T(8,128)(2,1)} async-done(((bf16[1600,1344]{1,0:T(8,128)(2,1)}), bf16[200,1344]{1,0:T(8,128)(2,1)}) %reduce-scatter.25.cloned.1.call-update) | async-done | bytes 537616
  1088.1 8.1 all-to-all-done.5
  1101.7 132.7 %reduce-scatter.29.cloned.1.call-done = bf16[200,1600]{1,0:T(8,128)(2,1)} async-done(((bf16[1600,1600]{1,0:T(8,128)(2,1)}), bf16[200,1600]{1,0:T(8,128)(2,1)}) %reduce-scatter.29.cloned.1.call-update) | async-done | bytes 640016
  1236.7 123.5 %reduce-scatter.27.cloned.1.call-done = bf16[200,1600]{1,0:T(8,128)(2,1)} async-done(((bf16[1600,1600]{1,0:T(8,128)(2,1)}), bf16[200,1600]{1,0:T(8,128)(2,1)}) %reduce-scatter.27.cloned.1.call-update) | async-done | bytes 640016
  1364.8 29.2 %psum.15 = f32[2944]{0:T(1024)S(1)} all-reduce(f32[2944]{0:T(1024)S(1)} %pad_maximum_fusion.8), channel_id=1, replica_groups=mesh['row'=8,'col'=4] {'row'}, use_global_device_ids=true, to_apply=%region_45.46 | all-reduce | flops 2944 | bytes 23552 | tf_op jit(solution)/shard_map/psum | solution.py:248
  1402.4 46.0 %psum.14 = f32[6,1600]{1,0:T(8,128)S(1)} all-reduce(f32[6,1600]{1,0:T(8,128)S(1)} %stack.110), channel_id=1, replica_groups=mesh['row'=8,'col'=4] {'row','col'}, use_global_device_ids=true, to_apply=%region_41.42 | all-reduce | flops 9600 | bytes 76800 | tf_op jit(solution)/shard_map/psum | solution.py:246
  (329 shorter events, 162.9 us)
Async XLA Ops:
  7.2 233.7 %all-gather.11.cloned.1.call-start = ((), (), s32[]{:S(2)}) async-start(), calls=%async_computation.16 | async-start | bytes 5068800 | tf_op jit(solution)/shard_map/all_gather | solution.py:142
  23.3 225.2 %all-gather.13.cloned.1.call-start = ((), (), s32[]{:S(2)}) async-start(), calls=%async_computation.17 | async-start | bytes 8192000 | tf_op jit(solution)/shard_map/all_gather | solution.py:187
  24.2 167.4 %copy-start.49 = (bf16[200,400]{1,0:T(8,128)(2,1)S(1)}, bf16[200,400]{1,0:T(8,128)(2,1)}, u32[]{:S(2)}) copy-start(bf16[200,400]{1,0:T(8,128)(2,1)} %param.19) | copy-start | bytes 480004
  85.4 126.9 %copy-start.42 = (f32[200]{0:T(256)S(1)}, f32[200]{0:T(256)}, u32[]{:S(2)}) copy-start(f32[200]{0:T(256)} %param.15) | copy-start | bytes 2404
  85.4 126.9 %copy-start.43 = (f32[200]{0:T(256)S(1)}, f32[200]{0:T(256)}, u32[]{:S(2)}) copy-start(f32[200]{0:T(256)} %param.16) | copy-start | bytes 2404
  85.4 126.9 %copy-start.44 = (f32[200]{0:T(256)S(1)}, f32[200]{0:T(256)}, u32[]{:S(2)}) copy-start(f32[200]{0:T(256)} %param.20) | copy-start | bytes 2404
  85.4 126.9 %copy-start.45 = (f32[200]{0:T(256)S(1)}, f32[200]{0:T(256)}, u32[]{:S(2)}) copy-start(f32[200]{0:T(256)} %param.21) | copy-start | bytes 2404
  85.4 126.9 %copy-start.46 = (f32[200]{0:T(256)S(1)}, f32[200]{0:T(256)}, u32[]{:S(2)}) copy-start(f32[200]{0:T(256)} %param.22) | copy-start | bytes 2404
  85.4 126.9 %copy-start.47 = (f32[200]{0:T(256)S(1)}, f32[200]{0:T(256)}, u32[]{:S(2)}) copy-start(f32[200]{0:T(256)} %param.26) | copy-start | bytes 2404
  85.6 104.9 %collective-permute-start = (bf16[2,1600,256]{2,1,0:T(8,128)(2,1)S(1)}, bf16[2,1600,256]{2,1,0:T(8,128)(2,1)S(1)}, u32[]{:S(2)}, u32[]{:S(2)}) collective-permute-start(bf16[2,1600,256]{2,1,0:T(8,128)(2,1)S(1)} %bitcast.483), channel_id=1, source_target_pairs={{0,0},{1,8},{2,16},{3,24},{4,1},{5,9},{6,17},{7,25},{8,2},{9,10},{... | collective-permute-start | bytes 4915208 | tf_op jit(solution)/shard_map/ppermute | solution.py:48
  193.0 46.9 %all-to-all-start.1 = ((bf16[200,4,112]{2,0,1:T(8,128)(2,1)}), bf16[200,4,112]{2,0,1:T(8,128)(2,1)S(1)}, u32[]{:S(2)}, u32[]{:S(2)}) async-start(bf16[200,4,112]{2,0,1:T(8,128)(2,1)} %copy.108), calls=%async_computation.1 | async-start | bytes 409600 | tf_op jit(solution)/shard_map/all_to_all | solution.py:72
  199.0 89.8 %all-gather.9.cloned.1.call-start = ((), (), s32[]{:S(2)}) async-start(), calls=%async_computation.15 | async-start | bytes 1843200 | tf_op jit(solution)/shard_map/all_gather | solution.py:142
  240.9 90.4 %reduce-scatter.15.cloned.1.call-start = ((), (), s32[]{:S(2)}) async-start(), calls=%async_computation.18 | async-start | bytes 4096000 | tf_op jit(solution)/shard_map/reduce_scatter | solution.py:136
  293.9 125.8 %all-gather.17.cloned.1.call-start = ((), (), s32[]{:S(2)}) async-start(), calls=%async_computation.20 | async-start | bytes 5990400 | tf_op jit(solution)/shard_map/all_gather | solution.py:142
  294.5 156.3 %all-gather.15.cloned.1.call-start = ((), (), s32[]{:S(2)}) async-start(), calls=%async_computation.19 | async-start | bytes 4096000 | tf_op jit(solution)/shard_map/all_gather | solution.py:132
  337.5 201.9 %all-gather.19.cloned.1.call-start = ((), (), s32[]{:S(2)}) async-start(), calls=%async_computation.21 | async-start | bytes 5990400 | tf_op jit(solution)/shard_map/all_gather | solution.py:142
  338.3 201.1 %copy-start.50 = (f32[1600]{0:T(1024)S(1)}, f32[1600]{0:T(1024)}, u32[]{:S(2)}) copy-start(f32[1600]{0:T(1024)} %param.24) | copy-start | bytes 19204
  338.3 264.4 %reduce-scatter.19.cloned.1.call-start = ((), (), s32[]{:S(2)}) async-start(), calls=%async_computation.23 | async-start | bytes 4096000 | tf_op jit(solution)/shard_map/reduce_scatter | solution.py:136
  564.5 73.6 %all-gather.21.cloned.1.call-start = ((), (), s32[]{:S(2)}) async-start(), calls=%async_computation.24 | async-start | bytes 4096000 | tf_op jit(solution)/shard_map/all_gather | solution.py:132
  608.2 129.1 %reduce-scatter.21.cloned.1.call-start = ((), (), s32[]{:S(2)}) async-start(), calls=%async_computation.25 | async-start | bytes 4096000 | tf_op jit(solution)/shard_map/reduce_scatter | solution.py:136
  686.9 80.4 %reduce-scatter.17.cloned.1.call-start = ((), (), s32[]{:S(2)}) async-start(), calls=%async_computation.22 | async-start | bytes 4096000 | tf_op jit(solution)/shard_map/reduce_scatter | solution.py:136
  698.5 173.3 %reduce-scatter.23.cloned.1.call-start = ((), (), s32[]{:S(2)}) async-start(), calls=%async_computation.26 | async-start | bytes 1843200 | tf_op jit(solution)/shard_map/reduce_scatter | solution.py:146
  703.9 377.2 %reduce-scatter.25.cloned.1.call-start = ((), (), s32[]{:S(2)}) async-start(), calls=%async_computation.27 | async-start | bytes 5068800
  713.7 520.7 %reduce-scatter.29.cloned.1.call-start = ((), (), s32[]{:S(2)}) async-start(), calls=%async_computation.29 | async-start | bytes 5990400
  726.9 633.3 %reduce-scatter.27.cloned.1.call-start = ((), (), s32[]{:S(2)}) async-start(), calls=%async_computation.28 | async-start | bytes 5990400
  771.9 107.9 %collective-permute-start.1 = (bf16[1600,256]{1,0:T(8,128)(2,1)}, bf16[1600,256]{1,0:T(8,128)(2,1)}, u32[]{:S(2)}, u32[]{:S(2)}) collective-permute-start(bf16[1600,256]{1,0:T(8,128)(2,1)} %get-tuple-element.34), channel_id=1, source_target_pairs={{0,0},{8,1},{16,2},{24,3},{1,4},{9,5},{17,6},{25,7},{2,8},{10,9},{... | collective-permute-start | bytes 2457608 | tf_op jit(solution)/shard_map/ppermute | solution.py:53
  879.8 204.3 %all-to-all-start.3 = ((bf16[8,200,1,256]{3,1,2,0:T(8,128)(2,1)}), bf16[8,200,1,256]{3,1,2,0:T(8,128)(2,1)S(1)}, u32[]{:S(2)}, u32[]{:S(2)}) async-start(bf16[8,200,1,256]{3,1,2,0:T(8,128)(2,1)} %bitcast.65), calls=%async_computation.5 | async-start | bytes 1638400 | tf_op jit(solution)/shard_map/all_to_all | solution.py:56
  884.4 203.7 %collective-permute-start.2 = (f32[1600,256]{1,0:T(8,128)}, f32[1600,256]{1,0:T(8,128)}, u32[]{:S(2)}, u32[]{:S(2)}) collective-permute-start(f32[1600,256]{1,0:T(8,128)} %get-tuple-element.33), channel_id=1, source_target_pairs={{0,0},{8,1},{16,2},{24,3},{1,4},{9,5},{17,6},{25,7},{2,8},{10,9},{... | collective-permute-start | bytes 4915208 | tf_op jit(solution)/shard_map/ppermute | solution.py:53
  1084.1 12.2 all-to-all-start.5
  1097.1 357.2 %all-to-all-start.4 = ((f32[8,200,1,256]{3,1,2,0:T(8,128)}), f32[8,200,1,256]{3,1,2,0:T(8,128)S(1)}, u32[]{:S(2)}, u32[]{:S(2)}) async-start(f32[8,200,1,256]{3,1,2,0:T(8,128)} %bitcast.120), calls=%async_computation.8 | async-start | bytes 3276800 | tf_op jit(solution)/shard_map/all_to_all | solution.py:56
  1101.7 263.1 %copy-start.34 = (f32[1600]{0:T(1024)S(1)}, f32[1600]{0:T(1024)}, u32[]{:S(2)}) copy-start(f32[1600]{0:T(1024)} %get-tuple-element.76) | copy-start | bytes 19204
  1101.7 299.5 %copy-start.33 = (s32[400]{0:T(512)S(1)}, s32[400]{0:T(512)}, u32[]{:S(2)}) copy-start(s32[400]{0:T(512)} %copy-done.32) | copy-start | bytes 4804
  (45 other events, 693.4 us)
Sparse Core Ops, SparseCore 0:
  23.4 148.3 all-gather.10
  191.8 49.7 all-gather.12
  244.3 44.4 all-gather.8
  294.0 37.1 reduce-scatter.14
  333.5 86.1 all-gather.16
  421.8 28.9 all-gather.14
  453.2 86.1 all-gather.18
  564.6 38.0 reduce-scatter.18
  608.3 29.6 all-gather.20
  687.0 38.7 reduce-scatter.20
  728.5 38.7 reduce-scatter.16
  770.6 101.1 reduce-scatter.22
  875.7 205.4 reduce-scatter.24
  1084.8 149.5 reduce-scatter.28
  1237.8 122.3 reduce-scatter.26
where the time goes:
time: 1470 us; the launch traced here: 1460 us
  waiting for transfers between devices  986 us (67%)
  blocking collectives  198 us (13%)
  matrix products  146 us (10%)
  other arithmetic  45.3 us (3%)
  local copies, waits for them, and re-layouts  40.1 us (3%)
  starting transfers between devices  31.4 us (2%)
  between operations  16.2 us (1%)
    unnamed x18, waiting for transfers between devices  450 us
    all_gather x4, waiting for transfers between devices, whole_weight(): return lax.all_gather(weight, 'row', axis=0, tiled=True)  167 us
    dot_general x58, matrix products, product(): lax.dot_general(left, right, dims, preferred_element_type=jnp.float32)  146 us
    ppermute x1, waiting for transfers between devices, to_blocks(): return lax.ppermute(got, ('row', 'col'), block_order(rows, cols))  103 us
    reduce_scatter x4, waiting for transfers between devices, share(): lax.psum_scatter(values.astype(jnp.bfloat16), 'col', scatter_dimension=1,...  102 us
    reduce_scatter x1, waiting for transfers between devices, share_weight(): lax.psum_scatter(gradient.astype(jnp.bfloat16), 'row', scatter_dimension=...  95.2 us
    all_to_all x1, blocking collectives, to_blocks(): got = lax.all_to_all(split, 'row', split_axis=2, concat_axis=1)  61.1 us
    all_gather x2, waiting for transfers between devices, spread(): return lax.all_gather(values, 'col', axis=1, tiled=True)  60.6 us
  transfers between devices with their start and end apart: 22, of which 14 were waited for; matrix products, arithmetic and copies ran while one was open for 9% of the time, Pallas kernels for 0%

commit v1 on v0

--- a/solution.py
+++ b/solution.py
@@ -13,6 +13,27 @@
 TN = (((0,), (0,)), ((), ()))
 NN = (((1,), (0,)), ((), ()))
 NT = (((1,), (1,)), ((), ()))
+
+
+def gather_around(x, axis, dim):
+    peers, here, extent = (lax.axis_size(axis), lax.axis_index(axis), x.shape[dim])
+    right = [(i, (i + 1) % peers) for i in range(peers)]
+    backward = [(i, (i - 1) % peers) for i in range(peers)]
+    out = jnp.zeros((*x.shape[:dim], peers * extent, *x.shape[dim + 1 :]), x.dtype)
+    out = lax.dynamic_update_slice_in_dim(out, x, here * extent, axis=dim)
+    from_left = from_right = x
+    middle = peers // 2
+    for step in range(1, middle + 1):
+        from_left = lax.ppermute(from_left, axis, right)
+        out = lax.dynamic_update_slice_in_dim(
+            out, from_left, (here - step) % peers * extent, axis=dim
+        )
+        if step < peers - middle:
+            from_right = lax.ppermute(from_right, axis, backward)
+            out = lax.dynamic_update_slice_in_dim(
+                out, from_right, (here + step) % peers * extent, axis=dim
+            )
+    return out
 
 
 def product(left, right, dims):
@@ -139,7 +160,7 @@
 
 
 def whole_weight(weight):
-    return lax.all_gather(weight, "row", axis=0, tiled=True)
+    return gather_around(weight, "row", 0)
 
 
 def share_weight(gradient):

time: 1470 us -> 1630 us (1.11)
  local copies, waits for them, and re-layouts: 40.1 us -> 135 us
  starting transfers between devices: 31.4 us -> 74 us
  waiting for transfers between devices: 986 us -> 1010 us
    ppermute x0 -> x28, waiting for transfers between devices: none -> 248 us  [the longest x12 154 us: gather_around(): from_right = lax.ppermute(from_right, axis, backward)]
    all_gather x4 -> x0, waiting for transfers between devices: 167 us -> none  [whole_weight(): return lax.all_gather(weight, 'row', axis=0, tiled=True)]
    dynamic_update_slice x0 -> x32, local copies, waits for them, and re-layouts: none -> 85.7 us  [the longest x16 41.9 us: gather_around(): lax.dynamic_update_slice_in_dim(out, from_left, (here - step) % peers * e...]
    ppermute x0 -> x28, starting transfers between devices: none -> 42.8 us  [the longest x12 25.8 us: gather_around(): from_right = lax.ppermute(from_right, axis, backward)]
    all_gather x2, waiting for transfers between devices: 60.6 us -> 29.3 us  [spread(): return lax.all_gather(values, 'col', axis=1, tiled=True)]
    ppermute x1, waiting for transfers between devices: 103 us -> 71.3 us  [to_blocks(): return lax.ppermute(got, ('row', 'col'), block_order(rows, cols))]
    all_to_all x1, blocking collectives: 61.1 us -> 42.8 us  [to_blocks(): got = lax.all_to_all(split, 'row', split_axis=2, concat_axis=1)]
    unnamed x18 -> x14, waiting for transfers between devices: 450 us -> 450 us
  transfers between devices with their start and end apart: 22 -> 46, of which waited for: 14 -> 22; matrix products, arithmetic and copies ran while one was open for 9% -> 11% of each run, Pallas kernels for 0% -> 0%
where the time goes in v1:
time: 1630 us; the launch traced here: 1620 us
  waiting for transfers between devices  1010 us (62%)
  blocking collectives  193 us (12%)
  matrix products  147 us (9%)
  local copies, waits for them, and re-layouts  135 us (8%)
  starting transfers between devices  74 us (5%)
  other arithmetic  45 us (3%)
  between operations  16.3 us (1%)
    unnamed x14, waiting for transfers between devices  450 us
    ppermute x12, waiting for transfers between devices, gather_around(): from_right = lax.ppermute(from_right, axis, backward)  154 us
    dot_general x58, matrix products, product(): lax.dot_general(left, right, dims, preferred_element_type=jnp.float32)  147 us
    reduce_scatter x4, waiting for transfers between devices, share(): lax.psum_scatter(values.astype(jnp.bfloat16), 'col', scatter_dimension=1,...  107 us
    reduce_scatter x1, waiting for transfers between devices, share_weight(): lax.psum_scatter(gradient.astype(jnp.bfloat16), 'row', scatter_dimension=...  95.4 us
    ppermute x16, waiting for transfers between devices, gather_around(): from_left = lax.ppermute(from_left, axis, right)  93.9 us
    ppermute x1, waiting for transfers between devices, to_blocks(): return lax.ppermute(got, ('row', 'col'), block_order(rows, cols))  71.3 us
    psum x1, blocking collectives, body(): features = lax.psum(features, ('row', 'col'))  46 us
  transfers between devices with their start and end apart: 46, of which 22 were waited for; matrix products, arithmetic and copies ran while one was open for 11% of the time, Pallas kernels for 0%

profile of v1, /device:TPU:14, one launch (start us, length us, event | category | flops | bytes accessed | tf_op | source)
XLA Modules:
  0.0 1620.5 jit_solution(14455313976478105312)
XLA Ops:
  10.5 42.8 %all_to_all.65 = bf16[2,1,200,8,256]{4,2,0,1,3:T(8,128)(2,1)S(1)} all-to-all(bf16[2,1,200,8,256]{4,2,0,1,3:T(8,128)(2,1)S(1)} %copy.120), channel_id=1, replica_groups=mesh['row'=8,'col'=4] {'row'}, dimensions={3} | all-to-all | bytes 3276800 | tf_op jit(solution)/shard_map/all_to_all | solution.py:67
  55.7 71.3 %collective-permute-done = bf16[2,1600,256]{2,1,0:T(8,128)(2,1)S(1)} collective-permute-done((bf16[2,1600,256]{2,1,0:T(8,128)(2,1)S(1)}, bf16[2,1600,256]{2,1,0:T(8,128)(2,1)S(1)}, u32[]{:S(2)}, u32[]{:S(2)}) %collective-permute-start) | collective-permute-done | bytes 1638432 | tf_op jit(solution)/shard_map/ppermute | solution.py:69
  131.2 22.6 %all_to_all.66 = bf16[200,4,336]{2,0,1:T(8,128)(2,1)S(1)} all-to-all(bf16[200,4,336]{2,0,1:T(8,128)(2,1)S(1)} %copy.124), channel_id=1, replica_groups=mesh['row'=8,'col'=4] {'col'}, dimensions={1} | all-to-all | bytes 1075200 | tf_op jit(solution)/shard_map/all_to_all | solution.py:93
  156.5 25.6 %collective-permute-done.8 = bf16[200,1344]{1,0:T(8,128)(2,1)S(1)} collective-permute-done((bf16[200,1344]{1,0:T(8,128)(2,1)S(1)}, bf16[200,1344]{1,0:T(8,128)(2,1)S(1)}, u32[]{:S(2)}, u32[]{:S(2)}) %collective-permute-start.8) | collective-permute-done | bytes 537632 | tf_op jit(solution)/shard_map/ppermute | solution.py:27
  191.0 30.3 %all-gather = f32[8,200,6]{1,2,0:T(8,128)S(1)} all-gather(f32[1,200,6]{1,2,0:T(8,128)S(1)} %bitcast.490), channel_id=1, replica_groups=mesh['row'=8,'col'=4] {'row'}, dimensions={0}, use_global_device_ids=true | all-gather | bytes 43200 | tf_op jit(solution)/shard_map/all_gather | solution.py:191
  223.0 10.2 all-reduce.1
  242.6 28.8 %collective-permute-done.2 = bf16[200,448]{1,0:T(8,128)(2,1)} collective-permute-done((bf16[200,448]{1,0:T(8,128)(2,1)S(1)}, bf16[200,448]{1,0:T(8,128)(2,1)}, u32[]{:S(2)}, u32[]{:S(2)}) %collective-permute-start.2) | collective-permute-done | bytes 179232 | tf_op jit(solution)/shard_map/ppermute | solution.py:32
  294.4 16.1 collective-permute-done.5
  312.3 14.5 collective-permute-done.7
  431.3 40.7 %reduce-scatter.15.cloned.1.call-done = bf16[1600,256]{1,0:T(8,128)(2,1)} async-done(((bf16[1600,1024]{1,0:T(8,128)(2,1)}), bf16[1600,256]{1,0:T(8,128)(2,1)}) %reduce-scatter.15.cloned.1.call-update) | async-done | bytes 819216 | tf_op jit(solution)/shard_map/reduce_scatter | solution.py:157
  491.3 31.4 %collective-permute-done.23 = bf16[200,1600]{1,0:T(8,128)(2,1)S(1)} collective-permute-done((bf16[200,1600]{1,0:T(8,128)(2,1)S(1)}, bf16[200,1600]{1,0:T(8,128)(2,1)S(1)}, u32[]{:S(2)}, u32[]{:S(2)}) %collective-permute-start.23) | collective-permute-done | bytes 640032 | tf_op jit(solution)/shard_map/ppermute | solution.py:32
  526.1 25.1 %collective-permute-done.16 = bf16[200,1600]{1,0:T(8,128)(2,1)S(1)} collective-permute-done((bf16[200,1600]{1,0:T(8,128)(2,1)S(1)}, bf16[200,1600]{1,0:T(8,128)(2,1)S(1)}, u32[]{:S(2)}, u32[]{:S(2)}) %collective-permute-start.16) | collective-permute-done | bytes 640032 | tf_op jit(solution)/shard_map/ppermute | solution.py:32
  558.2 21.5 %collective-permute-done.25 = bf16[200,1600]{1,0:T(8,128)(2,1)S(1)} collective-permute-done((bf16[200,1600]{1,0:T(8,128)(2,1)S(1)}, bf16[200,1600]{1,0:T(8,128)(2,1)S(1)}, u32[]{:S(2)}, u32[]{:S(2)}) %collective-permute-start.25) | collective-permute-done | bytes 640032 | tf_op jit(solution)/shard_map/ppermute | solution.py:32
  583.1 25.1 %collective-permute-done.18 = bf16[200,1600]{1,0:T(8,128)(2,1)S(1)} collective-permute-done((bf16[200,1600]{1,0:T(8,128)(2,1)S(1)}, bf16[200,1600]{1,0:T(8,128)(2,1)S(1)}, u32[]{:S(2)}, u32[]{:S(2)}) %collective-permute-start.18) | collective-permute-done | bytes 640032 | tf_op jit(solution)/shard_map/ppermute | solution.py:32
  615.2 23.4 %collective-permute-done.26 = bf16[200,1600]{1,0:T(8,128)(2,1)S(1)} collective-permute-done((bf16[200,1600]{1,0:T(8,128)(2,1)S(1)}, bf16[200,1600]{1,0:T(8,128)(2,1)S(1)}, u32[]{:S(2)}, u32[]{:S(2)}) %collective-permute-start.26) | collective-permute-done | bytes 640032 | tf_op jit(solution)/shard_map/ppermute | solution.py:27
  639.1 13.8 collective-permute-done.19
  656.0 22.4 %collective-permute-done.20 = bf16[200,1600]{1,0:T(8,128)(2,1)S(1)} collective-permute-done((bf16[200,1600]{1,0:T(8,128)(2,1)S(1)}, bf16[200,1600]{1,0:T(8,128)(2,1)S(1)}, u32[]{:S(2)}, u32[]{:S(2)}) %collective-permute-start.20) | collective-permute-done | bytes 640032 | tf_op jit(solution)/shard_map/ppermute | solution.py:32
  681.5 9.8 fusion.226
  691.4 17.0 %convert_reduce_fusion.1 = (f32[1600]{0:T(1024)}, bf16[1600,1024]{1,0:T(8,128)(2,1)S(1)}) fusion(f32[1600,1024]{1,0:T(8,128)S(1)} %fusion.226, f32[1600]{0:T(1024)S(1)} %copy-done.53, bf16[1600,1600]{1,0:T(8,128)(2,1)} %constant_dynamic-update-slice_fusion.22, bf16[2,1600,1024]{2,1,0:T(8,128)(2,1)} %all-gather.5.cloned.1.call-done), kind=kOutput, calls=%fused_computation.25 | convolution fusion | flops 5280561664 | bytes 18444800 | tf_op jit(solution)/shard_map/dot_general | solution.py:40
  710.2 10.1 convolution_convert_fusion.4
  720.6 39.1 %reduce-scatter.19.cloned.1.call-done = bf16[1600,256]{1,0:T(8,128)(2,1)} async-done(((bf16[1600,1024]{1,0:T(8,128)(2,1)}), bf16[1600,256]{1,0:T(8,128)(2,1)}) %reduce-scatter.19.cloned.1.call-update) | async-done | bytes 819216 | tf_op jit(solution)/shard_map/reduce_scatter | solution.py:157
  765.8 29.3 %all-gather.9.cloned.1.call-done = bf16[1600,1024]{1,0:T(8,128)(2,1)} async-done(((bf16[1600,256]{1,0:T(8,128)(2,1)}), bf16[1600,1024]{1,0:T(8,128)(2,1)}) %all-gather.9.cloned.1.call-update) | async-done | bytes 3276816 | tf_op jit(solution)/shard_map/all_gather | solution.py:153
  843.9 11.5 convolution_convert_fusion.5
  871.3 13.0 convolution_convert_fusion
  884.4 10.2 convolution_convert_fusion.1
  897.0 27.3 %reduce-scatter.17.cloned.1.call-done = bf16[1600,256]{1,0:T(8,128)(2,1)} async-done(((bf16[1600,1024]{1,0:T(8,128)(2,1)}), bf16[1600,256]{1,0:T(8,128)(2,1)}) %reduce-scatter.17.cloned.1.call-update) | async-done | bytes 819216 | tf_op jit(solution)/shard_map/reduce_scatter | solution.py:157
  933.6 95.4 %reduce-scatter.23.cloned.1.call-done = bf16[200,448]{1,0:T(8,128)(2,1)} async-done(((bf16[1600,448]{1,0:T(8,128)(2,1)}), bf16[200,448]{1,0:T(8,128)(2,1)}) %reduce-scatter.23.cloned.1.call-update) | async-done | bytes 179216 | tf_op jit(solution)/shard_map/reduce_scatter | solution.py:167
  1046.0 192.3 %reduce-scatter.25.cloned.1.call-done = bf16[200,1344]{1,0:T(8,128)(2,1)} async-done(((bf16[1600,1344]{1,0:T(8,128)(2,1)}), bf16[200,1344]{1,0:T(8,128)(2,1)}) %reduce-scatter.25.cloned.1.call-update) | async-done | bytes 537616
  1258.9 132.7 %reduce-scatter.29.cloned.1.call-done = bf16[200,1600]{1,0:T(8,128)(2,1)} async-done(((bf16[1600,1600]{1,0:T(8,128)(2,1)}), bf16[200,1600]{1,0:T(8,128)(2,1)}) %reduce-scatter.29.cloned.1.call-update) | async-done | bytes 640016
  1393.8 124.5 %reduce-scatter.27.cloned.1.call-done = bf16[200,1600]{1,0:T(8,128)(2,1)} async-done(((bf16[1600,1600]{1,0:T(8,128)(2,1)}), bf16[200,1600]{1,0:T(8,128)(2,1)}) %reduce-scatter.27.cloned.1.call-update) | async-done | bytes 640016
  1522.9 29.2 %psum.15 = f32[2944]{0:T(1024)S(1)} all-reduce(f32[2944]{0:T(1024)S(1)} %pad_maximum_fusion.8), channel_id=1, replica_groups=mesh['row'=8,'col'=4] {'row'}, use_global_device_ids=true, to_apply=%region_45.46 | all-reduce | flops 2944 | bytes 23552 | tf_op jit(solution)/shard_map/psum | solution.py:269
  1560.5 46.0 %psum.14 = f32[6,1600]{1,0:T(8,128)S(1)} all-reduce(f32[6,1600]{1,0:T(8,128)S(1)} %stack.110), channel_id=1, replica_groups=mesh['row'=8,'col'=4] {'row','col'}, use_global_device_ids=true, to_apply=%region_41.42 | all-reduce | flops 9600 | bytes 76800 | tf_op jit(solution)/shard_map/psum | solution.py:267
  (424 shorter events, 350.9 us)
Async XLA Ops:
  7.2 387.5 %all-gather.5.cloned.1.call-start = ((), (), s32[]{:S(2)}) async-start(), calls=%async_computation.15 | async-start | bytes 8192000 | tf_op jit(solution)/shard_map/all_gather | solution.py:208
  53.4 73.6 %collective-permute-start = (bf16[2,1600,256]{2,1,0:T(8,128)(2,1)S(1)}, bf16[2,1600,256]{2,1,0:T(8,128)(2,1)S(1)}, u32[]{:S(2)}, u32[]{:S(2)}) collective-permute-start(bf16[2,1600,256]{2,1,0:T(8,128)(2,1)S(1)} %bitcast.453), channel_id=1, source_target_pairs={{0,0},{1,8},{2,16},{3,24},{4,1},{5,9},{6,17},{7,25},{8,2},{9,10},{... | collective-permute-start | bytes 4915208 | tf_op jit(solution)/shard_map/ppermute | solution.py:69
  154.5 79.0 %collective-permute-start.9 = (bf16[200,1344]{1,0:T(8,128)(2,1)S(1)}, bf16[200,1344]{1,0:T(8,128)(2,1)}, u32[]{:S(2)}, u32[]{:S(2)}) collective-permute-start(bf16[200,1344]{1,0:T(8,128)(2,1)S(1)} %reshape.542), channel_id=1, source_target_pairs={{0,28},{4,0},{8,4},{12,8},{16,12},{20,16},{24,20},{28,24},{1,29},{... | collective-permute-start | bytes 1612808 | tf_op jit(solution)/shard_map/ppermute | solution.py:32
  182.2 56.3 %collective-permute-start.10 = (bf16[200,1344]{1,0:T(8,128)(2,1)S(1)}, bf16[200,1344]{1,0:T(8,128)(2,1)}, u32[]{:S(2)}, u32[]{:S(2)}) collective-permute-start(bf16[200,1344]{1,0:T(8,128)(2,1)S(1)} %collective-permute-done.8), channel_id=1, source_target_pairs={{0,4},{4,8},{8,12},{12,16},{16,20},{20,24},{24,28},{28,0},{1,5},{5... | collective-permute-start | bytes 1612808 | tf_op jit(solution)/shard_map/ppermute | solution.py:27
  185.5 53.1 %all-to-all-start.1 = ((bf16[200,4,112]{2,0,1:T(8,128)(2,1)}), bf16[200,4,112]{2,0,1:T(8,128)(2,1)S(1)}, u32[]{:S(2)}, u32[]{:S(2)}) async-start(bf16[200,4,112]{2,0,1:T(8,128)(2,1)} %copy.122), calls=%async_computation.1 | async-start | bytes 409600 | tf_op jit(solution)/shard_map/all_to_all | solution.py:93
  190.9 281.1 %reduce-scatter.15.cloned.1.call-start = ((), (), s32[]{:S(2)}) async-start(), calls=%async_computation.16 | async-start | bytes 4096000 | tf_op jit(solution)/shard_map/reduce_scatter | solution.py:157
  233.5 57.0 %collective-permute-start.11 = (bf16[200,1344]{1,0:T(8,128)(2,1)}, bf16[200,1344]{1,0:T(8,128)(2,1)}, u32[]{:S(2)}, u32[]{:S(2)}) collective-permute-start(bf16[200,1344]{1,0:T(8,128)(2,1)} %collective-permute-done.9), channel_id=1, source_target_pairs={{0,28},{4,0},{8,4},{12,8},{16,12},{20,16},{24,20},{28,24},{1,29},{... | collective-permute-start | bytes 1612808 | tf_op jit(solution)/shard_map/ppermute | solution.py:32
  238.5 53.9 %collective-permute-start.12 = (bf16[200,1344]{1,0:T(8,128)(2,1)}, bf16[200,1344]{1,0:T(8,128)(2,1)}, u32[]{:S(2)}, u32[]{:S(2)}) collective-permute-start(bf16[200,1344]{1,0:T(8,128)(2,1)} %collective-permute-done.10), channel_id=1, source_target_pairs={{0,4},{4,8},{8,12},{12,16},{16,20},{20,24},{24,28},{28,0},{1,5},{5... | collective-permute-start | bytes 1612808 | tf_op jit(solution)/shard_map/ppermute | solution.py:27
  290.5 84.3 %collective-permute-start.13 = (bf16[200,1344]{1,0:T(8,128)(2,1)}, bf16[200,1344]{1,0:T(8,128)(2,1)}, u32[]{:S(2)}, u32[]{:S(2)}) collective-permute-start(bf16[200,1344]{1,0:T(8,128)(2,1)} %collective-permute-done.11), channel_id=1, source_target_pairs={{0,28},{4,0},{8,4},{12,8},{16,12},{20,16},{24,20},{28,24},{1,29},{... | collective-permute-start | bytes 1612808 | tf_op jit(solution)/shard_map/ppermute | solution.py:32
  292.4 92.4 %collective-permute-start.14 = (bf16[200,1344]{1,0:T(8,128)(2,1)}, bf16[200,1344]{1,0:T(8,128)(2,1)}, u32[]{:S(2)}, u32[]{:S(2)}) collective-permute-start(bf16[200,1344]{1,0:T(8,128)(2,1)} %collective-permute-done.12), channel_id=1, source_target_pairs={{0,4},{4,8},{8,12},{12,16},{16,20},{20,24},{24,28},{28,0},{1,5},{5... | collective-permute-start | bytes 1612808 | tf_op jit(solution)/shard_map/ppermute | solution.py:27
  431.2 250.3 %all-gather.7.cloned.1.call-start = ((), (), s32[]{:S(2)}) async-start(), calls=%async_computation.17 | async-start | bytes 4096000 | tf_op jit(solution)/shard_map/all_gather | solution.py:153
  478.0 281.8 %reduce-scatter.19.cloned.1.call-start = ((), (), s32[]{:S(2)}) async-start(), calls=%async_computation.19 | async-start | bytes 4096000 | tf_op jit(solution)/shard_map/reduce_scatter | solution.py:157
  481.2 70.0 %collective-permute-start.16 = (bf16[200,1600]{1,0:T(8,128)(2,1)S(1)}, bf16[200,1600]{1,0:T(8,128)(2,1)S(1)}, u32[]{:S(2)}, u32[]{:S(2)}) collective-permute-start(bf16[200,1600]{1,0:T(8,128)(2,1)S(1)} %copy-done.27), channel_id=1, source_target_pairs={{0,28},{4,0},{8,4},{12,8},{16,12},{20,16},{24,20},{28,24},{1,29},{... | collective-permute-start | bytes 1920008 | tf_op jit(solution)/shard_map/ppermute | solution.py:32
  481.2 72.5 %collective-permute-start.15 = (bf16[200,1600]{1,0:T(8,128)(2,1)S(1)}, bf16[200,1600]{1,0:T(8,128)(2,1)S(1)}, u32[]{:S(2)}, u32[]{:S(2)}) collective-permute-start(bf16[200,1600]{1,0:T(8,128)(2,1)S(1)} %copy-done.27), channel_id=1, source_target_pairs={{0,4},{4,8},{8,12},{12,16},{16,20},{20,24},{24,28},{28,0},{1,5},{5... | collective-permute-start | bytes 1920008 | tf_op jit(solution)/shard_map/ppermute | solution.py:27
  522.7 57.1 %collective-permute-start.25 = (bf16[200,1600]{1,0:T(8,128)(2,1)S(1)}, bf16[200,1600]{1,0:T(8,128)(2,1)S(1)}, u32[]{:S(2)}, u32[]{:S(2)}) collective-permute-start(bf16[200,1600]{1,0:T(8,128)(2,1)S(1)} %collective-permute-done.23), channel_id=1, source_target_pairs={{0,28},{4,0},{8,4},{12,8},{16,12},{20,16},{24,20},{28,24},{1,29},{... | collective-permute-start | bytes 1920008 | tf_op jit(solution)/shard_map/ppermute | solution.py:32
  525.2 57.1 %collective-permute-start.24 = (bf16[200,1600]{1,0:T(8,128)(2,1)S(1)}, bf16[200,1600]{1,0:T(8,128)(2,1)S(1)}, u32[]{:S(2)}, u32[]{:S(2)}) collective-permute-start(bf16[200,1600]{1,0:T(8,128)(2,1)S(1)} %collective-permute-done.22), channel_id=1, source_target_pairs={{0,4},{4,8},{8,12},{12,16},{16,20},{20,24},{24,28},{28,0},{1,5},{5... | collective-permute-start | bytes 1920008 | tf_op jit(solution)/shard_map/ppermute | solution.py:27
  551.2 57.1 %collective-permute-start.18 = (bf16[200,1600]{1,0:T(8,128)(2,1)S(1)}, bf16[200,1600]{1,0:T(8,128)(2,1)S(1)}, u32[]{:S(2)}, u32[]{:S(2)}) collective-permute-start(bf16[200,1600]{1,0:T(8,128)(2,1)S(1)} %collective-permute-done.16), channel_id=1, source_target_pairs={{0,28},{4,0},{8,4},{12,8},{16,12},{20,16},{24,20},{28,24},{1,29},{... | collective-permute-start | bytes 1920008 | tf_op jit(solution)/shard_map/ppermute | solution.py:32
  553.7 57.1 %collective-permute-start.17 = (bf16[200,1600]{1,0:T(8,128)(2,1)S(1)}, bf16[200,1600]{1,0:T(8,128)(2,1)S(1)}, u32[]{:S(2)}, u32[]{:S(2)}) collective-permute-start(bf16[200,1600]{1,0:T(8,128)(2,1)S(1)} %collective-permute-done.15), channel_id=1, source_target_pairs={{0,4},{4,8},{8,12},{12,16},{16,20},{20,24},{24,28},{28,0},{1,5},{5... | collective-permute-start | bytes 1920008 | tf_op jit(solution)/shard_map/ppermute | solution.py:27
  579.7 75.4 %collective-permute-start.27 = (bf16[200,1600]{1,0:T(8,128)(2,1)S(1)}, bf16[200,1600]{1,0:T(8,128)(2,1)S(1)}, u32[]{:S(2)}, u32[]{:S(2)}) collective-permute-start(bf16[200,1600]{1,0:T(8,128)(2,1)S(1)} %collective-permute-done.25), channel_id=1, source_target_pairs={{0,28},{4,0},{8,4},{12,8},{16,12},{20,16},{24,20},{28,24},{1,29},{... | collective-permute-start | bytes 1920008 | tf_op jit(solution)/shard_map/ppermute | solution.py:32
  582.2 56.4 %collective-permute-start.26 = (bf16[200,1600]{1,0:T(8,128)(2,1)S(1)}, bf16[200,1600]{1,0:T(8,128)(2,1)S(1)}, u32[]{:S(2)}, u32[]{:S(2)}) collective-permute-start(bf16[200,1600]{1,0:T(8,128)(2,1)S(1)} %collective-permute-done.24), channel_id=1, source_target_pairs={{0,4},{4,8},{8,12},{12,16},{16,20},{20,24},{24,28},{28,0},{1,5},{5... | collective-permute-start | bytes 1920008 | tf_op jit(solution)/shard_map/ppermute | solution.py:27
  608.3 70.2 %collective-permute-start.20 = (bf16[200,1600]{1,0:T(8,128)(2,1)S(1)}, bf16[200,1600]{1,0:T(8,128)(2,1)S(1)}, u32[]{:S(2)}, u32[]{:S(2)}) collective-permute-start(bf16[200,1600]{1,0:T(8,128)(2,1)S(1)} %collective-permute-done.18), channel_id=1, source_target_pairs={{0,28},{4,0},{8,4},{12,8},{16,12},{20,16},{24,20},{28,24},{1,29},{... | collective-permute-start | bytes 1920008 | tf_op jit(solution)/shard_map/ppermute | solution.py:32
  720.3 74.8 %all-gather.9.cloned.1.call-start = ((), (), s32[]{:S(2)}) async-start(), calls=%async_computation.20 | async-start | bytes 4096000 | tf_op jit(solution)/shard_map/all_gather | solution.py:153
  765.3 129.4 %reduce-scatter.21.cloned.1.call-start = ((), (), s32[]{:S(2)}) async-start(), calls=%async_computation.21 | async-start | bytes 4096000 | tf_op jit(solution)/shard_map/reduce_scatter | solution.py:157
  843.9 80.4 %reduce-scatter.17.cloned.1.call-start = ((), (), s32[]{:S(2)}) async-start(), calls=%async_computation.18 | async-start | bytes 4096000 | tf_op jit(solution)/shard_map/reduce_scatter | solution.py:157
  855.5 173.5 %reduce-scatter.23.cloned.1.call-start = ((), (), s32[]{:S(2)}) async-start(), calls=%async_computation.22 | async-start | bytes 1843200 | tf_op jit(solution)/shard_map/reduce_scatter | solution.py:167
  861.0 377.3 %reduce-scatter.25.cloned.1.call-start = ((), (), s32[]{:S(2)}) async-start(), calls=%async_computation.23 | async-start | bytes 5068800
  870.8 520.7 %reduce-scatter.29.cloned.1.call-start = ((), (), s32[]{:S(2)}) async-start(), calls=%async_computation.25 | async-start | bytes 5990400
  884.3 633.9 %reduce-scatter.27.cloned.1.call-start = ((), (), s32[]{:S(2)}) async-start(), calls=%async_computation.24 | async-start | bytes 5990400
  929.0 108.1 %collective-permute-start.29 = (bf16[1600,256]{1,0:T(8,128)(2,1)}, bf16[1600,256]{1,0:T(8,128)(2,1)}, u32[]{:S(2)}, u32[]{:S(2)}) collective-permute-start(bf16[1600,256]{1,0:T(8,128)(2,1)} %get-tuple-element.34), channel_id=1, source_target_pairs={{0,0},{8,1},{16,2},{24,3},{1,4},{9,5},{17,6},{25,7},{2,8},{10,9},{... | collective-permute-start | bytes 2457608 | tf_op jit(solution)/shard_map/ppermute | solution.py:74
  1037.0 204.3 %all-to-all-start.3 = ((bf16[8,200,1,256]{3,1,2,0:T(8,128)(2,1)}), bf16[8,200,1,256]{3,1,2,0:T(8,128)(2,1)S(1)}, u32[]{:S(2)}, u32[]{:S(2)}) async-start(bf16[8,200,1,256]{3,1,2,0:T(8,128)(2,1)} %bitcast.63), calls=%async_computation.5 | async-start | bytes 1638400 | tf_op jit(solution)/shard_map/all_to_all | solution.py:77
  1041.6 203.8 %collective-permute-start.30 = (f32[1600,256]{1,0:T(8,128)}, f32[1600,256]{1,0:T(8,128)}, u32[]{:S(2)}, u32[]{:S(2)}) collective-permute-start(f32[1600,256]{1,0:T(8,128)} %get-tuple-element.33), channel_id=1, source_target_pairs={{0,0},{8,1},{16,2},{24,3},{1,4},{9,5},{17,6},{25,7},{2,8},{10,9},{... | collective-permute-start | bytes 4915208 | tf_op jit(solution)/shard_map/ppermute | solution.py:74
  1254.3 358.1 %all-to-all-start.4 = ((f32[8,200,1,256]{3,1,2,0:T(8,128)}), f32[8,200,1,256]{3,1,2,0:T(8,128)S(1)}, u32[]{:S(2)}, u32[]{:S(2)}) async-start(f32[8,200,1,256]{3,1,2,0:T(8,128)} %bitcast.116), calls=%async_computation.8 | async-start | bytes 3276800 | tf_op jit(solution)/shard_map/all_to_all | solution.py:77
  (73 other events, 2697.7 us)
Sparse Core Ops, SparseCore 0:
  128.3 60.4 all-gather.4
  431.4 40.6 reduce-scatter.14
  478.1 29.6 all-gather.6
  720.4 39.3 reduce-scatter.18
  765.4 29.6 all-gather.8
  844.0 38.7 reduce-scatter.20
  885.6 38.7 reduce-scatter.16
  927.8 101.2 reduce-scatter.22
  1032.9 205.3 reduce-scatter.24
  1242.0 149.5 reduce-scatter.28
  1395.0 123.1 reduce-scatter.26
